TPU v7x, 256 devices: a whole 4x4x8 slice. The times are simulated.
256 devices in a mesh: dp: 4 (over x), expert: 64 (over y, z, core).
Axes of the slice: x: 4, y: 4, z: 8, core: 2. Of those that a mesh axis runs over, the one named last changes fastest.
Arguments:
- frames: bfloat16 [32768, 1024], P(('dp', 'expert')), may hold values from -6 to 6
- lengths: int32 [256], P(('dp', 'expert')), may hold values from 64 to 128
- expert_ids: int32 [32768, 2], P(('dp', 'expert')), may hold values from 0 to 63, all different within a row
- conv_in: bfloat16 [1024, 2048], P(('dp', 'expert')), may hold values from -0.1875 to 0.1875
- depthwise: bfloat16 [1024, 31], P(('dp', 'expert')), may hold values from -1 to 1
- router: bfloat16 [1024, 64], P(('dp', 'expert')), may hold values from -0.1875 to 0.1875
- w_in: bfloat16 [64, 1024, 4096], P('expert', None, 'dp'), may hold values from -0.1875 to 0.1875
- w_out: bfloat16 [64, 4096, 1024], P('expert', 'dp'), may hold values from -0.09375 to 0.09375
- out_grad: bfloat16 [32768, 1024], P(('dp', 'expert')), may hold values from -6 to 6
Outputs:
- layer_out: bfloat16 [32768, 1024], P(('dp', 'expert'))
- frames_grad: bfloat16 [32768, 1024], P(('dp', 'expert'))
- conv_in_grad: float32 [1024, 2048], P(('dp', 'expert'))
- depthwise_grad: float32 [1024, 31], P(('dp', 'expert'))
- router_grad: float32 [1024, 64], P(('dp', 'expert'))
- w_in_grad: bfloat16 [64, 1024, 4096], P('expert', None, 'dp')
- w_out_grad: bfloat16 [64, 4096, 1024], P('expert', 'dp')
Inputs may be any that keep to these rules, and one draw needn't show every extreme that they name: `expert_ids`: each frame names 2 different experts, and every expert is named by some frame.
All inputs are finite; a program needn't handle non-finite values.
Results may differ from a plain program's by a relative error of at most 0.019.
Values may be sent and summed in bfloat16 or wider, within the bound.
A program may use at most 128 MiB of HBM per device.

v0:
```python
import jax
import jax.numpy as jnp
from jax import lax
from jax.sharding import PartitionSpec as P

TOP = 2
KERNEL = 31
EPSILON = 1e-05


def swish_of(values):
    return values * jax.nn.sigmoid(values)


def swish_slope(values):
    sigmoid_v = jax.nn.sigmoid(values)
    return sigmoid_v * (1.0 + values * (1.0 - sigmoid_v))


def normalize(values):
    center = values - jnp.mean(values, axis=-1, keepdims=True)
    inv_scale = lax.rsqrt(jnp.mean(center * center, axis=-1, keepdims=True) + EPSILON)
    return (center * inv_scale, inv_scale)


def norm_backward(upstream, centred, inv_scale):
    first_mean = jnp.mean(upstream, axis=-1, keepdims=True)
    second_mean = jnp.mean(upstream * centred, axis=-1, keepdims=True)
    return inv_scale * (upstream - first_mean - centred * second_mean)


def pad_time(signal, half_width):
    return jnp.pad(signal, ((half_width, half_width), (0, 0)))


def depth_apply(signal, tap_rows, half_width):
    length = signal.shape[0]
    padded = pad_time(signal, half_width)
    summed = jnp.zeros(signal.shape, jnp.float32)
    for tap_index in range(tap_rows.shape[0]):
        summed = summed + tap_rows[tap_index] * lax.slice_in_dim(
            padded, tap_index, tap_index + length, axis=0
        )
    return summed


def depth_transpose(upstream, tap_rows, half_width):
    length = upstream.shape[0]
    padded = pad_time(upstream, half_width)
    summed = jnp.zeros(upstream.shape, jnp.float32)
    for tap_index in range(tap_rows.shape[0]):
        begin = 2 * half_width - tap_index
        summed = summed + tap_rows[tap_index] * lax.slice_in_dim(
            padded, begin, begin + length, axis=0
        )
    return summed


def depth_taps_grad(upstream, signal, half_width):
    length = signal.shape[0]
    padded = pad_time(signal, half_width)
    rows_list = []
    for tap_index in range(2 * half_width + 1):
        piece = lax.slice_in_dim(padded, tap_index, tap_index + length, axis=0)
        rows_list.append(jnp.sum(upstream * piece, axis=0))
    return jnp.stack(rows_list, axis=0)


def routing(choices, length, experts, capacity):
    tokens, top_count = choices.shape
    usable = jnp.arange(tokens, dtype=jnp.int32) < length
    flat_ids = choices.reshape(-1)
    live = jnp.repeat(usable, top_count)
    onehot = (flat_ids[:, None] == jnp.arange(experts, dtype=jnp.int32)[None, :]) & live[:, None]
    onehot_int = onehot.astype(jnp.int32)
    before = jnp.cumsum(onehot_int, axis=0) - onehot_int
    position = jnp.sum(jnp.where(onehot, before, 0), axis=1)
    kept_rows = live & (position < capacity)
    slot_total = experts * capacity
    slot_index = jnp.where(kept_rows, flat_ids * capacity + position, slot_total)
    match = slot_index[None, :] == jnp.arange(slot_total, dtype=jnp.int32)[:, None]
    filled = jnp.any(match, axis=1)
    source = jnp.sum(
        jnp.where(match, jnp.arange(tokens * top_count, dtype=jnp.int32)[None, :], 0), axis=1
    )
    return (usable, kept_rows, jnp.minimum(slot_index, slot_total - 1), filled, source)


def dispatch(send_rows):
    arrived_cols = lax.all_to_all(send_rows, "expert", split_axis=0, concat_axis=0, tiled=True)
    arrived = lax.all_gather(arrived_cols[None], "dp", axis=0, tiled=True)
    return arrived.reshape(-1, send_rows.shape[-1])


def collect(term_maker, rows_here, columns, capacity, width):
    summed = lax.psum_scatter(
        term_maker(jnp.int32(0), rows_here * lax.axis_size("dp")).astype(jnp.bfloat16),
        "dp",
        scatter_dimension=0,
        tiled=True,
    )
    returned = lax.all_to_all(
        summed.reshape(columns, capacity, width), "expert", split_axis=0, concat_axis=0, tiled=True
    )
    return returned.reshape(columns * capacity, width)


def per_device(frames, lengths, expert_ids, conv_in, depthwise, router, w_in, w_out, out_grad):
    tokens, width = frames.shape
    experts = router.shape[1]
    capacity = TOP * tokens // experts
    columns = lax.axis_size("expert")
    rows_here = columns * capacity
    half_width = (KERNEL - 1) // 2
    conv_full, depth_full, router_full = (
        lax.all_gather(conv_in, ("dp", "expert"), axis=0, tiled=True),
        lax.all_gather(depthwise, ("dp", "expert"), axis=0, tiled=True),
        lax.all_gather(router, ("dp", "expert"), axis=0, tiled=True),
    )
    usable, kept_rows, slot_index, filled, source = routing(
        expert_ids, lengths[0], experts, capacity
    )
    frame_mask = usable.astype(jnp.float32)[:, None]
    frame_wide = frames.astype(jnp.float32)
    centred, inv_scale = normalize(frame_wide)
    normed = centred.astype(jnp.bfloat16)
    pointwise = jnp.dot(normed, conv_full, preferred_element_type=jnp.float32)
    value_half = pointwise[:, :width]
    gate_sig = jax.nn.sigmoid(pointwise[:, width:])
    gated = value_half * gate_sig * frame_mask
    tap_rows = depth_full.astype(jnp.float32).T
    conv_sum = depth_apply(gated, tap_rows, half_width)
    mixed_rows = (frame_wide + swish_of(conv_sum) * frame_mask).astype(jnp.bfloat16)
    logits = jnp.dot(mixed_rows, router_full, preferred_element_type=jnp.float32)
    onehots = (expert_ids[:, :, None] == jnp.arange(experts, dtype=jnp.int32)).astype(jnp.float32)
    chosen = jnp.sum(logits[:, None, :] * onehots, axis=-1)
    scores = jax.nn.sigmoid(chosen)
    score_sum = jnp.sum(scores, axis=-1, keepdims=True)
    weights = scores / score_sum
    kept_wide = kept_rows.reshape(tokens, TOP).astype(jnp.float32)
    send_rows = jnp.take(mixed_rows, source // TOP, axis=0)
    send_rows = jnp.where(filled[:, None], send_rows, jnp.zeros((), jnp.bfloat16)).reshape(
        experts, capacity, width
    )
    slot_rows = dispatch(send_rows)
    hidden = jnp.dot(slot_rows, w_in[0], preferred_element_type=jnp.float32)
    active = swish_of(hidden).astype(jnp.bfloat16)

    def forward_term(start, count):
        partial_rows = jnp.dot(active, w_out[0], preferred_element_type=jnp.float32).astype(
            jnp.bfloat16
        )
        return lax.optimization_barrier(partial_rows).astype(jnp.float32)

    expert_rows = collect(forward_term, rows_here, columns, capacity, width)
    picked = jnp.take(expert_rows, slot_index, axis=0).reshape(tokens, TOP, width)
    picked_wide = picked.astype(jnp.float32) * kept_wide[..., None]
    layer_out = (
        mixed_rows.astype(jnp.float32) + jnp.sum(weights[..., None] * picked_wide, axis=1)
    ).astype(jnp.bfloat16)
    conv_back, depth_back, router_back = (
        lax.all_gather(conv_in, ("dp", "expert"), axis=0, tiled=True),
        lax.all_gather(depthwise, ("dp", "expert"), axis=0, tiled=True),
        lax.all_gather(router, ("dp", "expert"), axis=0, tiled=True),
    )
    grad_wide = out_grad.astype(jnp.float32)
    weight_grad = jnp.sum(grad_wide[:, None, :] * picked_wide, axis=-1)
    mean_term = jnp.sum(weight_grad * weights, axis=-1, keepdims=True)
    chosen_grad = (weight_grad - mean_term) / score_sum * scores * (1.0 - scores)
    logit_grad = jnp.sum(chosen_grad[..., None] * onehots, axis=1).astype(jnp.bfloat16)
    router_part = lax.dot_general(
        mixed_rows, logit_grad, (((0,), (0,)), ((), ())), preferred_element_type=jnp.float32
    )
    router_term = lax.dot_general(
        logit_grad, router_back, (((1,), (1,)), ((), ())), preferred_element_type=jnp.float32
    )
    slot_cot = (
        ((weights * kept_wide)[..., None] * grad_wide[:, None, :])
        .astype(jnp.bfloat16)
        .reshape(tokens * TOP, width)
    )
    cot_send = jnp.take(slot_cot, source, axis=0)
    cot_send = jnp.where(filled[:, None], cot_send, jnp.zeros((), jnp.bfloat16)).reshape(
        experts, capacity, width
    )
    cot_rows = dispatch(cot_send)
    act_grad = lax.dot_general(
        cot_rows, w_out[0], (((1,), (1,)), ((), ())), preferred_element_type=jnp.float32
    )
    pre_grad = (act_grad * swish_slope(hidden)).astype(jnp.bfloat16)
    w_out_grad = lax.dot_general(
        active, cot_rows, (((0,), (0,)), ((), ())), preferred_element_type=jnp.float32
    ).astype(jnp.bfloat16)[None]
    w_in_grad = lax.dot_general(
        slot_rows, pre_grad, (((0,), (0,)), ((), ())), preferred_element_type=jnp.float32
    ).astype(jnp.bfloat16)[None]

    def backward_term(start, count):
        partial_rows = lax.dot_general(
            pre_grad, w_in[0], (((1,), (1,)), ((), ())), preferred_element_type=jnp.float32
        ).astype(jnp.bfloat16)
        return lax.optimization_barrier(partial_rows).astype(jnp.float32)

    back_rows = collect(backward_term, rows_here, columns, capacity, width)
    slot_grad = jnp.take(back_rows, slot_index, axis=0).reshape(tokens, TOP, width)
    slot_grad = slot_grad.astype(jnp.float32) * kept_wide[..., None]
    mixed_grad = grad_wide + jnp.sum(slot_grad, axis=1) + router_term
    conv_grad = mixed_grad * frame_mask * swish_slope(conv_sum)
    tap_back = depth_back.astype(jnp.float32).T
    glu_grad = depth_transpose(conv_grad, tap_back, half_width) * frame_mask
    taps_grad = depth_taps_grad(conv_grad, gated, half_width)
    value_grad = glu_grad * gate_sig
    gate_grad = glu_grad * value_half * gate_sig * (1.0 - gate_sig)
    pre_cot = jnp.concatenate([value_grad, gate_grad], axis=-1).astype(jnp.bfloat16)
    conv_part = lax.dot_general(
        normed, pre_cot, (((0,), (0,)), ((), ())), preferred_element_type=jnp.float32
    )
    normed_grad = lax.dot_general(
        pre_cot, conv_back, (((1,), (1,)), ((), ())), preferred_element_type=jnp.float32
    )
    frames_grad = (mixed_grad + norm_backward(normed_grad, centred, inv_scale)).astype(jnp.bfloat16)
    conv_in_grad, depthwise_grad, router_grad = (
        lax.psum_scatter(conv_part, ("dp", "expert"), scatter_dimension=0, tiled=True),
        lax.psum_scatter(taps_grad.T, ("dp", "expert"), scatter_dimension=0, tiled=True),
        lax.psum_scatter(router_part, ("dp", "expert"), scatter_dimension=0, tiled=True),
    )
    return (
        layer_out,
        frames_grad,
        conv_in_grad,
        depthwise_grad,
        router_grad,
        w_in_grad,
        w_out_grad,
    )


def solution(mesh):
    in_specs = (
        P(("dp", "expert"), None),
        P(("dp", "expert")),
        P(("dp", "expert"), None),
        P(("dp", "expert"), None),
        P(("dp", "expert"), None),
        P(("dp", "expert"), None),
        P("expert", None, "dp"),
        P("expert", "dp", None),
        P(("dp", "expert"), None),
    )
    out_specs = (
        P(("dp", "expert"), None),
        P(("dp", "expert"), None),
        P(("dp", "expert"), None),
        P(("dp", "expert"), None),
        P(("dp", "expert"), None),
        P("expert", None, "dp"),
        P("expert", "dp", None),
    )
    return jax.shard_map(
        per_device, mesh=mesh, in_specs=in_specs, out_specs=out_specs, check_vma=False
    )
```

profile of v0, /device:TPU:8, one launch (start us, length us, event | category | flops | bytes accessed | tf_op | source)
XLA Modules:
  0.0 790.0 jit_solution(2469328729457799150)
XLA Ops:
  11.9 65.2 %all-gather.2 = bf16[256,4,31]{2,1,0:T(4,128)(2,1)S(1)} all-gather(bf16[1,4,31]{2,1,0:T(4,128)(2,1)} %bitcast.231), channel_id=1, replica_groups=mesh['dp'=4,'expert'=64] {'dp','expert'}, dimensions={0}, use_global_device_ids=true | all-gather | bytes 63736 | tf_op jit(solution)/shard_map/all_gather | solution.py:117
  79.9 49.8 %all-gather.13.cloned.1.call-done = bf16[256,4,2048]{2,1,0:T(4,128)(2,1)} async-done(((bf16[1,4,2048]{2,1,0:T(4,128)(2,1)}), bf16[256,4,2048]{2,1,0:T(4,128)(2,1)}) %all-gather.13.cloned.1.call-update) | async-done | bytes 4194320 | tf_op jit(solution)/shard_map/all_gather | solution.py:116
  129.7 6.9 reshape.380
  147.5 24.6 %all_to_all.20 = bf16[64,4,1024]{2,1,0:T(4,128)(2,1)} all-to-all(bf16[64,4,1024]{2,1,0:T(4,128)(2,1)S(1)} %select_select_fusion.1), channel_id=1, replica_groups=mesh['dp'=4,'expert'=64] {'expert'}, dimensions={0} | all-to-all | bytes 1048576 | tf_op jit(solution)/shard_map/all_to_all | solution.py:90
  172.1 29.8 %all-gather.9.cloned.1.call-done = bf16[256,4,1024]{2,1,0:T(4,128)(2,1)} async-done(((bf16[64,4,1024]{2,1,0:T(4,128)(2,1)}), bf16[256,4,1024]{2,1,0:T(4,128)(2,1)}) %all-gather.9.cloned.1.call-update) | async-done | bytes 2097168 | tf_op jit(solution)/shard_map/all_gather | solution.py:91
  201.9 3.9 reshape.326
  205.8 4.5 fusion.5
  212.3 3.7 fusion.10
  216.1 32.4 %reduce-scatter.4.cloned.1.call-done = bf16[256,1024]{1,0:T(8,128)(2,1)} async-done(((bf16[1024,1024]{1,0:T(8,128)(2,1)}), bf16[256,1024]{1,0:T(8,128)(2,1)}) %reduce-scatter.4.cloned.1.call-update) | async-done | bytes 524304 | tf_op jit(solution)/shard_map/reduce_scatter | solution.py:96
  250.6 10.8 %all-to-all-start.1 = ((bf16[64,4,1024]{2,1,0:T(4,128)(2,1)}), bf16[64,4,1024]{2,1,0:T(4,128)(2,1)}, u32[]{:S(2)}, u32[]{:S(2)}) async-start(bf16[64,4,1024]{2,1,0:T(4,128)(2,1)} %reshape.327), calls=%async_computation.2 | async-start | bytes 1048576 | tf_op jit(solution)/shard_map/all_to_all | solution.py:102
  261.4 65.0 %all-gather.4 = bf16[256,4,64]{2,1,0:T(4,128)(2,1)S(1)} all-gather(bf16[1,4,64]{2,1,0:T(4,128)(2,1)S(1)} %bitcast.232), channel_id=1, replica_groups=mesh['dp'=4,'expert'=64] {'dp','expert'}, dimensions={0}, use_global_device_ids=true | all-gather | bytes 131584 | tf_op jit(solution)/shard_map/all_gather | solution.py:118
  342.3 25.9 %all_to_all.21 = bf16[64,4,1024]{2,1,0:T(4,128)(2,1)} all-to-all(bf16[64,4,1024]{2,1,0:T(4,128)(2,1)} %reshape.330), channel_id=1, replica_groups=mesh['dp'=4,'expert'=64] {'expert'}, dimensions={0} | all-to-all | bytes 1048576 | tf_op jit(solution)/shard_map/all_to_all | solution.py:90
  368.3 30.5 %all-gather.11.cloned.1.call-done = bf16[256,4,1024]{2,1,0:T(4,128)(2,1)} async-done(((bf16[64,4,1024]{2,1,0:T(4,128)(2,1)}), bf16[256,4,1024]{2,1,0:T(4,128)(2,1)}) %all-gather.11.cloned.1.call-update) | async-done | bytes 2097168 | tf_op jit(solution)/shard_map/all_gather | solution.py:91
  398.8 4.0 reshape.331
  402.8 6.1 multiply_convert_fusion
  410.2 3.7 fusion.7
  413.9 32.4 %reduce-scatter.6.cloned.1.call-done = bf16[256,1024]{1,0:T(8,128)(2,1)} async-done(((bf16[1024,1024]{1,0:T(8,128)(2,1)}), bf16[256,1024]{1,0:T(8,128)(2,1)}) %reduce-scatter.6.cloned.1.call-update) | async-done | bytes 524304 | tf_op jit(solution)/shard_map/reduce_scatter | solution.py:96
  448.4 10.6 %all-to-all-start.3 = ((bf16[64,4,1024]{2,1,0:T(4,128)(2,1)}), bf16[64,4,1024]{2,1,0:T(4,128)(2,1)S(1)}, u32[]{:S(2)}, u32[]{:S(2)}) async-start(bf16[64,4,1024]{2,1,0:T(4,128)(2,1)} %reshape.332), calls=%async_computation.5 | async-start | bytes 1048576 | tf_op jit(solution)/shard_map/all_to_all | solution.py:102
  460.4 15.3 %all-to-all-done.3 = bf16[64,4,1024]{2,1,0:T(4,128)(2,1)S(1)} async-done(((bf16[64,4,1024]{2,1,0:T(4,128)(2,1)}), bf16[64,4,1024]{2,1,0:T(4,128)(2,1)S(1)}, u32[]{:S(2)}, u32[]{:S(2)}) %all-to-all-start.3) | async-done | bytes 524320 | tf_op jit(solution)/shard_map/all_to_all | solution.py:102
  482.5 5.0 multiply_reduce_fusion.1
  494.6 4.6 fusion.89
  503.6 5.5 convert_bitcast_fusion.1
  509.0 3.8 convert_bitcast_fusion
  516.2 262.3 %all-reduce.8.cloned.1.call-done = (f32[1024,2048]{1,0:T(8,128)}, f32[1024,31]{0,1:T(8,128)}, f32[1024,64]{1,0:T(8,128)}) async-done(((f32[1024,2048]{1,0:T(8,128)}, f32[1024,31]{0,1:T(8,128)}, f32[1024,64]{1,0:T(8,128)}), (f32[1024,2048]{1,0:T(8,128)}, f32[1024,31]{0,1:T(8,128)}, f32[1024,64]{1,0:T(8,128)})) %all-reduce.8.cloned.1.call-update) | async-done | bytes 8777744
  (323 shorter events, 66.9 us)
Async XLA Ops:
  7.2 205.2 %copy-start = (bf16[1,1024,1024]{2,1,0:T(8,128)(2,1)S(1)}, bf16[1,1024,1024]{2,1,0:T(8,128)(2,1)}, u32[]{:S(2)}) copy-start(bf16[1,1024,1024]{2,1,0:T(8,128)(2,1)} %param.18) | copy-start | bytes 6291460
  7.2 122.5 %all-gather.13.cloned.1.call-start = ((), (), s32[]{:S(2)}) async-start(), calls=%async_computation.10 | async-start | bytes 4210688 | tf_op jit(solution)/shard_map/all_gather | solution.py:116
  7.9 193.9 %all-gather.9.cloned.1.call-start = ((), (), s32[]{:S(2)}) async-start(), calls=%async_computation.8 | async-start | bytes 2621440 | tf_op jit(solution)/shard_map/all_gather | solution.py:91
  11.2 322.9 %copy-start.87 = (pred[256]{0:T(512)(128)(4,1)}, pred[256]{0:T(512)(128)(4,1)S(1)}, u32[]{:S(2)}) copy-start(pred[256]{0:T(512)(128)(4,1)S(1)} %get-tuple-element.81) | copy-start | bytes 772
  77.2 63.4 %copy-start.85 = (f32[128]{0:T(128)}, f32[128]{0:T(128)S(1)}, u32[]{:S(2)}) copy-start(f32[128]{0:T(128)S(1)} %fusion.106) | copy-start | bytes 1540
  79.6 61.0 %copy-start.16 = (f32[1,1024]{1,0:T(1,128)}, f32[1,1024]{1,0:T(1,128)S(1)}, u32[]{:S(2)}) copy-start(f32[1,1024]{1,0:T(1,128)S(1)} %get-tuple-element.106) | copy-start | bytes 12292
  79.6 61.0 %copy-start.18 = (f32[1,1024]{1,0:T(1,128)}, f32[1,1024]{1,0:T(1,128)S(1)}, u32[]{:S(2)}) copy-start(f32[1,1024]{1,0:T(1,128)S(1)} %get-tuple-element.107) | copy-start | bytes 12292
  79.6 61.0 %copy-start.20 = (f32[1,1024]{1,0:T(1,128)}, f32[1,1024]{1,0:T(1,128)S(1)}, u32[]{:S(2)}) copy-start(f32[1,1024]{1,0:T(1,128)S(1)} %get-tuple-element.108) | copy-start | bytes 12292
  79.6 61.0 %copy-start.22 = (f32[1,1024]{1,0:T(1,128)}, f32[1,1024]{1,0:T(1,128)S(1)}, u32[]{:S(2)}) copy-start(f32[1,1024]{1,0:T(1,128)S(1)} %get-tuple-element.109) | copy-start | bytes 12292
  79.6 61.0 %copy-start.24 = (f32[1,1024]{1,0:T(1,128)}, f32[1,1024]{1,0:T(1,128)S(1)}, u32[]{:S(2)}) copy-start(f32[1,1024]{1,0:T(1,128)S(1)} %get-tuple-element.110) | copy-start | bytes 12292
  79.6 61.0 %copy-start.26 = (f32[1,1024]{1,0:T(1,128)}, f32[1,1024]{1,0:T(1,128)S(1)}, u32[]{:S(2)}) copy-start(f32[1,1024]{1,0:T(1,128)S(1)} %get-tuple-element.111) | copy-start | bytes 12292
  79.6 61.0 %copy-start.28 = (f32[1,1024]{1,0:T(1,128)}, f32[1,1024]{1,0:T(1,128)S(1)}, u32[]{:S(2)}) copy-start(f32[1,1024]{1,0:T(1,128)S(1)} %get-tuple-element.112) | copy-start | bytes 12292
  79.6 61.0 %copy-start.30 = (f32[1,1024]{1,0:T(1,128)}, f32[1,1024]{1,0:T(1,128)S(1)}, u32[]{:S(2)}) copy-start(f32[1,1024]{1,0:T(1,128)S(1)} %get-tuple-element.113) | copy-start | bytes 12292
  79.6 61.0 %copy-start.32 = (f32[1,1024]{1,0:T(1,128)}, f32[1,1024]{1,0:T(1,128)S(1)}, u32[]{:S(2)}) copy-start(f32[1,1024]{1,0:T(1,128)S(1)} %get-tuple-element.114) | copy-start | bytes 12292
  79.7 61.0 %copy-start.34 = (f32[1,1024]{1,0:T(1,128)}, f32[1,1024]{1,0:T(1,128)S(1)}, u32[]{:S(2)}) copy-start(f32[1,1024]{1,0:T(1,128)S(1)} %get-tuple-element.115) | copy-start | bytes 12292
  172.0 76.5 %reduce-scatter.4.cloned.1.call-start = ((), (), s32[]{:S(2)}) async-start(), calls=%async_computation.6 | async-start | bytes 2621440 | tf_op jit(solution)/shard_map/reduce_scatter | solution.py:96
  216.0 110.4 %copy-start.14 = (bf16[128,1024]{1,0:T(8,128)(2,1)S(1)}, bf16[128,1024]{1,0:T(8,128)(2,1)}, u32[]{:S(2)}) copy-start(bf16[128,1024]{1,0:T(8,128)(2,1)} %param.19) | copy-start | bytes 786436
  250.6 80.4 %all-to-all-start.1 = ((bf16[64,4,1024]{2,1,0:T(4,128)(2,1)}), bf16[64,4,1024]{2,1,0:T(4,128)(2,1)}, u32[]{:S(2)}, u32[]{:S(2)}) async-start(bf16[64,4,1024]{2,1,0:T(4,128)(2,1)} %reshape.327), calls=%async_computation.2 | async-start | bytes 1048576 | tf_op jit(solution)/shard_map/all_to_all | solution.py:102
  261.3 137.5 %all-gather.11.cloned.1.call-start = ((), (), s32[]{:S(2)}) async-start(), calls=%async_computation.9 | async-start | bytes 2621440 | tf_op jit(solution)/shard_map/all_gather | solution.py:91
  261.4 69.5 %copy-start.82 = (s32[128,2]{0,1:T(2,128)S(1)}, s32[128,2]{0,1:T(2,128)}, u32[]{:S(2)}) copy-start(s32[128,2]{0,1:T(2,128)} %param.13) | copy-start | bytes 3076
  368.2 78.1 %reduce-scatter.6.cloned.1.call-start = ((), (), s32[]{:S(2)}) async-start(), calls=%async_computation.7 | async-start | bytes 2621440 | tf_op jit(solution)/shard_map/reduce_scatter | solution.py:96
  448.4 27.3 %all-to-all-start.3 = ((bf16[64,4,1024]{2,1,0:T(4,128)(2,1)}), bf16[64,4,1024]{2,1,0:T(4,128)(2,1)S(1)}, u32[]{:S(2)}, u32[]{:S(2)}) async-start(bf16[64,4,1024]{2,1,0:T(4,128)(2,1)} %reshape.332), calls=%async_computation.5 | async-start | bytes 1048576 | tf_op jit(solution)/shard_map/all_to_all | solution.py:102
  459.0 319.6 %all-reduce.8.cloned.1.call-start = ((), (), s32[]{:S(2)}) async-start(), calls=%async_computation.11 | async-start | bytes 18087936
  512.9 269.9 %copy-start.1 = (bf16[1,1024,1024]{2,1,0:T(8,128)(2,1)S(1)}, bf16[1,1024,1024]{2,1,0:T(8,128)(2,1)}, u32[]{:S(2)}) copy-start(bf16[1,1024,1024]{2,1,0:T(8,128)(2,1)} %param.18) | copy-start | bytes 6291460
  (95 other events, 1864.5 us)
Sparse Core Ops, SparseCore 0:
  11.7 117.9 all-gather.12
  172.2 29.6 all-gather.8
  216.2 32.2 reduce-scatter.3
  368.4 30.4 all-gather.10
  414.1 32.2 reduce-scatter.5
  502.1 276.3 all-reduce.7
where the time goes:
time: 800 us; the launch traced here: 790 us
  waiting for transfers between devices  453 us (57%)
  blocking collectives  181 us (23%)
  local copies, waits for them, and re-layouts  52.2 us (7%)
  matrix products  40.9 us (5%)
  other arithmetic  24.6 us (3%)
  starting transfers between devices  21.6 us (3%)
  between operations  16.9 us (2%)
    unnamed x7, waiting for transfers between devices  263 us
    all_gather x1, blocking collectives, per_device(): lax.all_gather(depthwise, ('dp', 'expert'), axis=0, tiled=True)  65.2 us
    all_gather x1, blocking collectives, per_device(): lax.all_gather(router, ('dp', 'expert'), axis=0, tiled=True)  65 us
    reduce_scatter x2, waiting for transfers between devices, collect(): lax.psum_scatter(term_maker(jnp.int32(0), rows_here * lax.axis_size('dp')...  64.8 us
    all_gather x2, waiting for transfers between devices, dispatch(): arrived = lax.all_gather(arrived_cols[None], 'dp', axis=0, tiled=True)  60.3 us
    all_to_all x2, blocking collectives, dispatch(): lax.all_to_all(send_rows, 'expert', split_axis=0, concat_axis=0, tiled=True)  50.5 us
    all_gather x1, waiting for transfers between devices, per_device(): lax.all_gather(conv_in, ('dp', 'expert'), axis=0, tiled=True)  49.8 us
    all_to_all x2, starting transfers between devices, collect(): lax.all_to_all(summed.reshape(columns, capacity, width), 'expert', split_...  21.3 us
  transfers between devices with their start and end apart: 8, of which 7 were waited for; matrix products, arithmetic and copies ran while one was open for 3% of the time, Pallas kernels for 0%

commit v1 on v0

--- a/solution.py
+++ b/solution.py
@@ -106,6 +106,18 @@
 
 
 def per_device(frames, lengths, expert_ids, conv_in, depthwise, router, w_in, w_out, out_grad):
+
+    def vectors_map(mine):
+        return jnp.concatenate(
+            lax.all_to_all(
+                jnp.stack(lax.axis_size(("dp", "expert")) * [mine]),
+                axis_name=("dp", "expert"),
+                split_axis=0,
+                concat_axis=0,
+            ),
+            axis=0,
+        )
+
     tokens, width = frames.shape
     experts = router.shape[1]
     capacity = TOP * tokens // experts
@@ -114,7 +126,7 @@
     half_width = (KERNEL - 1) // 2
     conv_full, depth_full, router_full = (
         lax.all_gather(conv_in, ("dp", "expert"), axis=0, tiled=True),
-        lax.all_gather(depthwise, ("dp", "expert"), axis=0, tiled=True),
+        vectors_map(depthwise),
         lax.all_gather(router, ("dp", "expert"), axis=0, tiled=True),
     )
     usable, kept_rows, slot_index, filled, source = routing(

time: 800 us -> 829 us (1.036)
  starting transfers between devices: 21.6 us -> 34 us
  local copies, waits for them, and re-layouts: 52.2 us -> 63.8 us
    all_gather x1, waiting for transfers between devices: 49.8 us -> 82.2 us  [per_device(): lax.all_gather(conv_in, ('dp', 'expert'), axis=0, tiled=True)]
    reduce_scatter x2, waiting for transfers between devices: 64.8 us -> 32.4 us  [collect(): lax.psum_scatter(term_maker(jnp.int32(0), rows_here * lax.axis_size('dp')...]
    all_to_all x0 -> x1, starting transfers between devices: none -> 14.6 us  [vectors_map(): lax.all_to_all(jnp.stack(lax.axis_size(('dp', 'expert')) * [mine]), axis_...]
    all_to_all x0 -> x1, waiting for transfers between devices: none -> 8.75 us  [vectors_map(): lax.all_to_all(jnp.stack(lax.axis_size(('dp', 'expert')) * [mine]), axis_...]
    slice x2, local copies, waits for them, and re-layouts: 0.1 us -> 8.43 us  [depth_apply(): tap_rows[tap_index]]
    unnamed x228 -> x168, local copies, waits for them, and re-layouts: 17.9 us -> 18.5 us
  transfers between devices with their start and end apart: 8 -> 9, of which waited for: 7 -> 7; matrix products, arithmetic and copies ran while one was open for 3% -> 4% of each run, Pallas kernels for 0% -> 0%
where the time goes in v1:
time: 829 us; the launch traced here: 818 us
  waiting for transfers between devices  461 us (56%)
  blocking collectives  177 us (21%)
  local copies, waits for them, and re-layouts  63.8 us (8%)
  matrix products  41.1 us (5%)
  starting transfers between devices  34 us (4%)
  other arithmetic  24.5 us (3%)
  between operations  16.4 us (2%)
    unnamed x7, waiting for transfers between devices  264 us
    all_gather x1, waiting for transfers between devices, per_device(): lax.all_gather(conv_in, ('dp', 'expert'), axis=0, tiled=True)  82.2 us
    all_gather x1, blocking collectives, per_device(): lax.all_gather(router, ('dp', 'expert'), axis=0, tiled=True)  65 us
    all_gather x1, blocking collectives, per_device(): lax.all_gather(depthwise, ('dp', 'expert'), axis=0, tiled=True)  61 us
    all_gather x2, waiting for transfers between devices, dispatch(): arrived = lax.all_gather(arrived_cols[None], 'dp', axis=0, tiled=True)  60.1 us
    all_to_all x2, blocking collectives, dispatch(): lax.all_to_all(send_rows, 'expert', split_axis=0, concat_axis=0, tiled=True)  50.8 us
    reduce_scatter x2, waiting for transfers between devices, collect(): lax.psum_scatter(term_maker(jnp.int32(0), rows_here * lax.axis_size('dp')...  32.4 us
    all_to_all x2, starting transfers between devices, collect(): lax.all_to_all(summed.reshape(columns, capacity, width), 'expert', split_...  19 us
  transfers between devices with their start and end apart: 9, of which 7 were waited for; matrix products, arithmetic and copies ran while one was open for 4% of the time, Pallas kernels for 0%

profile of v1, /device:TPU:8, one launch (start us, length us, event | category | flops | bytes accessed | tf_op | source)
XLA Modules:
  0.0 818.2 jit_solution(10453811116927901489)
XLA Ops:
  9.4 14.6 %all-to-all-start = ((bf16[256,4,31]{2,1,0:T(4,128)(2,1)}), bf16[256,4,31]{2,1,0:T(4,128)(2,1)S(1)}, u32[]{:S(2)}, u32[]{:S(2)}) async-start(bf16[256,4,31]{2,1,0:T(4,128)(2,1)} %stack.66), calls=%async_computation | async-start | bytes 524288 | tf_op jit(solution)/shard_map/all_to_all | solution.py:112
  30.3 8.8 %all-to-all-done = bf16[256,4,31]{2,1,0:T(4,128)(2,1)S(1)} async-done(((bf16[256,4,31]{2,1,0:T(4,128)(2,1)}), bf16[256,4,31]{2,1,0:T(4,128)(2,1)S(1)}, u32[]{:S(2)}, u32[]{:S(2)}) %all-to-all-start) | async-done | bytes 63520 | tf_op jit(solution)/shard_map/all_to_all | solution.py:112
  42.4 5.1 slice_reduce_fusion.30
  47.5 82.2 %all-gather.13.cloned.1.call-done = bf16[256,4,2048]{2,1,0:T(4,128)(2,1)} async-done(((bf16[1,4,2048]{2,1,0:T(4,128)(2,1)}), bf16[256,4,2048]{2,1,0:T(4,128)(2,1)}) %all-gather.13.cloned.1.call-update) | async-done | bytes 4194320 | tf_op jit(solution)/shard_map/all_gather | solution.py:128
  129.8 6.9 reshape.384
  147.3 24.9 %all_to_all.25 = bf16[64,4,1024]{2,1,0:T(4,128)(2,1)} all-to-all(bf16[64,4,1024]{2,1,0:T(4,128)(2,1)S(1)} %select_select_fusion.1), channel_id=1, replica_groups=mesh['dp'=4,'expert'=64] {'expert'}, dimensions={0} | all-to-all | bytes 1048576 | tf_op jit(solution)/shard_map/all_to_all | solution.py:90
  172.3 29.8 %all-gather.9.cloned.1.call-done = bf16[256,4,1024]{2,1,0:T(4,128)(2,1)} async-done(((bf16[64,4,1024]{2,1,0:T(4,128)(2,1)}), bf16[256,4,1024]{2,1,0:T(4,128)(2,1)}) %all-gather.9.cloned.1.call-update) | async-done | bytes 2097168 | tf_op jit(solution)/shard_map/all_gather | solution.py:91
  202.0 3.9 reshape.331
  206.0 4.5 fusion.5
  216.3 32.4 %reduce-scatter.4.cloned.1.call-done = bf16[256,1024]{1,0:T(8,128)(2,1)} async-done(((bf16[1024,1024]{1,0:T(8,128)(2,1)}), bf16[256,1024]{1,0:T(8,128)(2,1)}) %reduce-scatter.4.cloned.1.call-update) | async-done | bytes 524304 | tf_op jit(solution)/shard_map/reduce_scatter | solution.py:96
  250.7 10.8 %all-to-all-start.2 = ((bf16[64,4,1024]{2,1,0:T(4,128)(2,1)}), bf16[64,4,1024]{2,1,0:T(4,128)(2,1)}, u32[]{:S(2)}, u32[]{:S(2)}) async-start(bf16[64,4,1024]{2,1,0:T(4,128)(2,1)} %reshape.332), calls=%async_computation.3 | async-start | bytes 1048576 | tf_op jit(solution)/shard_map/all_to_all | solution.py:102
  261.5 65.0 %all-gather.3 = bf16[256,4,64]{2,1,0:T(4,128)(2,1)S(1)} all-gather(bf16[1,4,64]{2,1,0:T(4,128)(2,1)S(1)} %bitcast.206), channel_id=1, replica_groups=mesh['dp'=4,'expert'=64] {'dp','expert'}, dimensions={0}, use_global_device_ids=true | all-gather | bytes 131584 | tf_op jit(solution)/shard_map/all_gather | solution.py:130
  342.4 25.9 %all_to_all.26 = bf16[64,4,1024]{2,1,0:T(4,128)(2,1)} all-to-all(bf16[64,4,1024]{2,1,0:T(4,128)(2,1)} %reshape.335), channel_id=1, replica_groups=mesh['dp'=4,'expert'=64] {'expert'}, dimensions={0} | all-to-all | bytes 1048576 | tf_op jit(solution)/shard_map/all_to_all | solution.py:90
  368.6 30.3 %all-gather.11.cloned.1.call-done = bf16[256,4,1024]{2,1,0:T(4,128)(2,1)} async-done(((bf16[64,4,1024]{2,1,0:T(4,128)(2,1)}), bf16[256,4,1024]{2,1,0:T(4,128)(2,1)}) %all-gather.11.cloned.1.call-update) | async-done | bytes 2097168 | tf_op jit(solution)/shard_map/all_gather | solution.py:91
  399.0 4.0 reshape.336
  403.0 6.1 multiply_convert_fusion
  414.7 61.0 %all-gather.4 = bf16[256,4,31]{2,1,0:T(4,128)(2,1)S(1)} all-gather(bf16[1,4,31]{2,1,0:T(4,128)(2,1)S(1)} %bitcast.204), channel_id=1, replica_groups=mesh['dp'=4,'expert'=64] {'dp','expert'}, dimensions={0}, use_global_device_ids=true | all-gather | bytes 63736 | tf_op jit(solution)/shard_map/all_gather | solution.py:175
  478.0 8.2 %all-to-all-start.4 = ((bf16[64,4,1024]{2,1,0:T(4,128)(2,1)}), bf16[64,4,1024]{2,1,0:T(4,128)(2,1)S(1)}, u32[]{:S(2)}, u32[]{:S(2)}) async-start(bf16[64,4,1024]{2,1,0:T(4,128)(2,1)} %reshape.337), calls=%async_computation.6 | async-start | bytes 1048576 | tf_op jit(solution)/shard_map/all_to_all | solution.py:102
  488.8 14.1 %all-to-all-done.4 = bf16[64,4,1024]{2,1,0:T(4,128)(2,1)S(1)} async-done(((bf16[64,4,1024]{2,1,0:T(4,128)(2,1)}), bf16[64,4,1024]{2,1,0:T(4,128)(2,1)S(1)}, u32[]{:S(2)}, u32[]{:S(2)}) %all-to-all-start.4) | async-done | bytes 524320 | tf_op jit(solution)/shard_map/all_to_all | solution.py:102
  509.8 5.0 multiply_reduce_fusion.1
  522.2 4.6 fusion.89
  531.1 5.4 convert_bitcast_fusion.1
  536.6 3.8 convert_bitcast_fusion
  543.7 263.0 %all-reduce.8.cloned.1.call-done = (f32[1024,2048]{1,0:T(8,128)}, f32[1024,31]{0,1:T(8,128)}, f32[1024,64]{1,0:T(8,128)}) async-done(((f32[1024,2048]{1,0:T(8,128)}, f32[1024,31]{0,1:T(8,128)}, f32[1024,64]{1,0:T(8,128)}), (f32[1024,2048]{1,0:T(8,128)}, f32[1024,31]{0,1:T(8,128)}, f32[1024,64]{1,0:T(8,128)})) %all-reduce.8.cloned.1.call-update) | async-done | bytes 8777744
  (269 shorter events, 81.2 us)
Async XLA Ops:
  7.2 205.3 %copy-start = (bf16[1,1024,1024]{2,1,0:T(8,128)(2,1)S(1)}, bf16[1,1024,1024]{2,1,0:T(8,128)(2,1)}, u32[]{:S(2)}) copy-start(bf16[1,1024,1024]{2,1,0:T(8,128)(2,1)} %param.18) | copy-start | bytes 6291460
  7.2 122.6 %all-gather.13.cloned.1.call-start = ((), (), s32[]{:S(2)}) async-start(), calls=%async_computation.11 | async-start | bytes 4210688 | tf_op jit(solution)/shard_map/all_gather | solution.py:128
  9.4 29.7 %all-to-all-start = ((bf16[256,4,31]{2,1,0:T(4,128)(2,1)}), bf16[256,4,31]{2,1,0:T(4,128)(2,1)S(1)}, u32[]{:S(2)}, u32[]{:S(2)}) async-start(bf16[256,4,31]{2,1,0:T(4,128)(2,1)} %stack.66), calls=%async_computation | async-start | bytes 524288 | tf_op jit(solution)/shard_map/all_to_all | solution.py:112
  24.0 178.1 %all-gather.9.cloned.1.call-start = ((), (), s32[]{:S(2)}) async-start(), calls=%async_computation.9 | async-start | bytes 2621440 | tf_op jit(solution)/shard_map/all_gather | solution.py:91
  27.3 307.0 %copy-start.56 = (pred[256]{0:T(512)(128)(4,1)}, pred[256]{0:T(512)(128)(4,1)S(1)}, u32[]{:S(2)}) copy-start(pred[256]{0:T(512)(128)(4,1)S(1)} %get-tuple-element.119) | copy-start | bytes 772
  28.8 107.9 %copy-start.16 = (f32[128]{0:T(128)}, f32[128]{0:T(128)S(1)}, u32[]{:S(2)}) copy-start(f32[128]{0:T(128)S(1)} %broadcast_multiply_fusion.2) | copy-start | bytes 1540
  30.0 106.7 %copy-start.49 = (f32[128]{0:T(128)}, f32[128]{0:T(128)S(1)}, u32[]{:S(2)}) copy-start(f32[128]{0:T(128)S(1)} %add_rsqrt_fusion) | copy-start | bytes 1540
  30.0 110.6 %copy-start.54 = (f32[128]{0:T(128)}, f32[128]{0:T(128)S(1)}, u32[]{:S(2)}) copy-start(f32[128]{0:T(128)S(1)} %fusion.106) | copy-start | bytes 1540
  47.5 89.2 %copy-start.3 = (bf16[128,1024]{1,0:T(8,128)(2,1)S(1)}, bf16[128,1024]{1,0:T(8,128)(2,1)}, u32[]{:S(2)}) copy-start(bf16[128,1024]{1,0:T(8,128)(2,1)} %param.11) | copy-start | bytes 786436
  172.2 76.5 %reduce-scatter.4.cloned.1.call-start = ((), (), s32[]{:S(2)}) async-start(), calls=%async_computation.7 | async-start | bytes 2621440 | tf_op jit(solution)/shard_map/reduce_scatter | solution.py:96
  216.2 45.3 %copy-start.76 = (bf16[4,64]{1,0:T(4,128)(2,1)S(1)}, bf16[4,64]{1,0:T(4,128)(2,1)}, u32[]{:S(2)}) copy-start(bf16[4,64]{1,0:T(4,128)(2,1)} %param.16) | copy-start | bytes 1540
  216.2 110.3 %copy-start.14 = (bf16[128,1024]{1,0:T(8,128)(2,1)S(1)}, bf16[128,1024]{1,0:T(8,128)(2,1)}, u32[]{:S(2)}) copy-start(bf16[128,1024]{1,0:T(8,128)(2,1)} %param.19) | copy-start | bytes 786436
  250.7 80.4 %all-to-all-start.2 = ((bf16[64,4,1024]{2,1,0:T(4,128)(2,1)}), bf16[64,4,1024]{2,1,0:T(4,128)(2,1)}, u32[]{:S(2)}, u32[]{:S(2)}) async-start(bf16[64,4,1024]{2,1,0:T(4,128)(2,1)} %reshape.332), calls=%async_computation.3 | async-start | bytes 1048576 | tf_op jit(solution)/shard_map/all_to_all | solution.py:102
  261.5 137.5 %all-gather.11.cloned.1.call-start = ((), (), s32[]{:S(2)}) async-start(), calls=%async_computation.10 | async-start | bytes 2621440 | tf_op jit(solution)/shard_map/all_gather | solution.py:91
  261.5 69.5 %copy-start.51 = (s32[128,2]{0,1:T(2,128)S(1)}, s32[128,2]{0,1:T(2,128)}, u32[]{:S(2)}) copy-start(s32[128,2]{0,1:T(2,128)} %param.13) | copy-start | bytes 3076
  368.4 107.6 %reduce-scatter.6.cloned.1.call-start = ((), (), s32[]{:S(2)}) async-start(), calls=%async_computation.8 | async-start | bytes 2621440 | tf_op jit(solution)/shard_map/reduce_scatter | solution.py:96
  403.0 7.4 copy-start.77
  414.1 73.6 %copy-start.75 = (f32[128]{0:T(128)S(1)}, f32[128]{0:T(128)}, u32[]{:S(2)}) copy-start(f32[128]{0:T(128)} %get-tuple-element.115) | copy-start | bytes 1540
  414.1 73.6 %copy-start.52 = (s32[128,2]{0,1:T(2,128)S(1)}, s32[128,2]{0,1:T(2,128)}, u32[]{:S(2)}) copy-start(s32[128,2]{0,1:T(2,128)} %param.13) | copy-start | bytes 3076
  478.0 24.9 %all-to-all-start.4 = ((bf16[64,4,1024]{2,1,0:T(4,128)(2,1)}), bf16[64,4,1024]{2,1,0:T(4,128)(2,1)S(1)}, u32[]{:S(2)}, u32[]{:S(2)}) async-start(bf16[64,4,1024]{2,1,0:T(4,128)(2,1)} %reshape.337), calls=%async_computation.6 | async-start | bytes 1048576 | tf_op jit(solution)/shard_map/all_to_all | solution.py:102
  486.3 320.5 %all-reduce.8.cloned.1.call-start = ((), (), s32[]{:S(2)}) async-start(), calls=%async_computation.12 | async-start | bytes 18087936
  531.1 5.5 copy-start.11
  531.1 5.5 copy-start.79
  540.4 270.6 %copy-start.1 = (bf16[1,1024,1024]{2,1,0:T(8,128)(2,1)S(1)}, bf16[1,1024,1024]{2,1,0:T(8,128)(2,1)}, u32[]{:S(2)}) copy-start(bf16[1,1024,1024]{2,1,0:T(8,128)(2,1)} %param.18) | copy-start | bytes 6291460
  (66 other events, 266.9 us)
Sparse Core Ops, SparseCore 0:
  11.7 117.9 all-gather.12
  172.3 29.6 all-gather.8
  216.4 32.2 reduce-scatter.3
  368.5 30.4 all-gather.10
  414.2 32.3 reduce-scatter.5
  529.7 277.0 all-reduce.7
